TPU v7x, 32 devices: a whole 2x2x4 slice. The times are simulated.
32 devices in a mesh: fsdp: 16 (over z, y, x), tp: 2 (over core).
Axes of the slice: x: 2, y: 2, z: 4, core: 2. Of those that a mesh axis runs over, the one named last changes fastest.
Arguments:
- tokens: bfloat16 [2, 16384, 512], P(None, ('fsdp', 'tp')), may hold values from -6 to 6
- gain_attn: float32 [512], replicated, may hold values from 0.5 to 1.5
- gain_ffn: float32 [512], replicated, may hold values from 0.5 to 1.5
- w_query: bfloat16 [512, 512], P('fsdp', 'tp'), may hold values from -0.25 to 0.25
- w_key: bfloat16 [512, 512], P('fsdp', 'tp'), may hold values from -0.25 to 0.25
- w_value: bfloat16 [512, 512], P('fsdp', 'tp'), may hold values from -0.25 to 0.25
- w_out: bfloat16 [512, 512], P('tp', 'fsdp'), may hold values from -0.75 to 0.75
- w_in: bfloat16 [512, 2048], P('fsdp', 'tp'), may hold values from -0.25 to 0.25
- w_down: bfloat16 [2048, 512], P('tp', 'fsdp'), may hold values from -0.125 to 0.125
- segment_ids: int32 [2, 512], P(None, 'fsdp'), may hold values from 0 to 4, as said below
- cotangent: bfloat16 [2, 16384, 512], P(None, ('fsdp', 'tp')), may hold values from -6 to 6
Outputs:
- result: bfloat16 [2, 16384, 512], P(None, ('fsdp', 'tp'))
- grad_tokens: bfloat16 [2, 16384, 512], P(None, ('fsdp', 'tp'))
- grad_gain_attn: float32 [512], P(('fsdp', 'tp'))
- grad_gain_ffn: float32 [512], P(('fsdp', 'tp'))
- grad_query: float32 [512, 512], P('fsdp', 'tp')
- grad_key: float32 [512, 512], P('fsdp', 'tp')
- grad_value: float32 [512, 512], P('fsdp', 'tp')
- grad_out: float32 [512, 512], P('tp', 'fsdp')
- grad_in: float32 [512, 2048], P('fsdp', 'tp')
- grad_down: float32 [2048, 512], P('tp', 'fsdp')
Inputs may be any that keep to these rules, and one draw needn't show every extreme that they name: `segment_ids`: within each group of 32 blocks of a micro-batch the ids never fall, begin with a prompt of 0s over a quarter to a half of the blocks, and every id 1 to 4 names a run of one block or more.
All inputs are finite; a program needn't handle non-finite values.
Results may differ from a plain program's by a relative error of at most 0.014.
Values may be sent and summed in bfloat16 or wider, within the bound.
A program may use at most 192 MiB of HBM per device.

v0:
```python
import collections
import functools
import math
import jax, jax.numpy as jnp
from jax import lax
from jax.experimental import pallas as pl
from jax.experimental.pallas import tpu as pltpu
from jax.sharding import PartitionSpec as P

F32, BF = jnp.float32, jnp.bfloat16
HI = lax.Precision.HIGHEST
HD, BLK, ITERS, NB, D, FF, T = 64, 32, 8, 32, 512, 2048, 1024
HALF = D // 2
COLS = 3 * HALF + HALF + FF
QO, KO, VO, OO, FO = 0, 256, 512, 768, 1024
UNITS = 512


def in_cols(u):
    return slice(FO + 2 * u * UNITS, FO + (2 * u + 1) * UNITS)


def down_cols(u):
    return slice(FO + (2 * u + 1) * UNITS, FO + (2 * u + 2) * UNITS)


def span(start, count):
    return pl.ds(pl.multiple_of(start, 128), count)


def nn(a, b, precision=None):
    return lax.dot_general(a, b, (((1,), (0,)), ((), ())), precision=precision, preferred_element_type=F32)


def nt(a, b, precision=None):
    return lax.dot_general(a, b, (((1,), (1,)), ((), ())), precision=precision, preferred_element_type=F32)


def tn(a, b, precision=None):
    return lax.dot_general(a, b, (((0,), (0,)), ((), ())), precision=precision, preferred_element_type=F32)


def iota(shape, dim):
    return lax.broadcasted_iota(jnp.int32, shape, dim)


def order_matrix(inverse):
    n, m = iota((128, 128), 0), iota((128, 128), 1)
    if inverse:
        n, m = m, n
    return (m == (n & 3) * 32 + (n >> 2)).astype(BF)


def norm_rows(x, gain):
    center = x - jnp.mean(x, axis=1, keepdims=True)
    inv = lax.rsqrt(jnp.mean(center * center, axis=1, keepdims=True) + 1e-05)
    xhat = center * inv
    return xhat, inv


def norm_back(xhat, inv, gain, grad):
    gx = grad * gain
    m1 = jnp.mean(gx, axis=1, keepdims=True)
    m2 = jnp.mean(gx * xhat, axis=1, keepdims=True)
    return inv * (gx - m1 - xhat * m2)


def even_lanes(shape):
    return (iota(shape, len(shape) - 1) & 127) < 64


def stack_heads(x):
    ev = even_lanes(x.shape)
    z = jnp.zeros_like(x)
    return jnp.concatenate([jnp.where(ev, x, z), jnp.where(ev, z, x)], axis=0)


def pick_heads(r):
    n = r.shape[0] // 2
    ev = even_lanes((n, r.shape[1]))
    return jnp.where(ev, r[:n], r[n:])


SCRATCH = dict(
    tokp=((T, D), BF), cotp=((T, D), BF), cott=((D, T), BF), nm=((T, D), BF), nmt=((D, T), BF),
    q=((T, D), BF), k=((T, D), BF), v=((T, D), BF), ks=((T, D), BF), vs=((T, D), BF),
    qm=((NB, D), F32), km=((NB, D), F32), sk=((2 * ITERS, 8 * NB, NB), F32), allow=((NB, NB), F32),
    kr=((8, 128, 128), BF), krt=((8, 128, 128), BF), hidq=((256, 128), BF), hidk=((256, 128), BF),
    pr=((4, 8, 256, 256), BF), mix=((T, D), BF), mid=((T, D), F32), nf=((T, D), BF), nft=((D, T), BF),
    hid=((T, UNITS), BF), gp=((T, UNITS), BF), res=((T, D), F32), gnf=((T, D), F32),
    ga=((T, D), BF), gat=((D, T), BF), gmix=((T, D), BF), dv=((T, D), F32), ds=((8 * NB, NB), F32),
    gg=((8, D), F32),
)
SHARED = dict(dq="res", dk="gnf", dks="hid", dvs="gp", dqb="ga", dkb="nm", dvb="nf")


def loop(n, body, unroll=1):
    lax.fori_loop(0, n, lambda i, c: (body(i), c)[1], 0, unroll=unroll)


def rows(i, n):
    return pl.ds(pl.multiple_of(i * n, n), n)


def pipeline(units, stages, lags, after=None):
    vals = [{} for _ in units]
    for step in range(len(units) + lags[-1]):
        for st, lag in reversed(list(zip(stages, lags))):
            if 0 <= step - lag < len(units):
                st(units[step - lag], vals[step - lag])
        if after is not None:
            after(step)


def st_tokens(s, tok, gain_attn):
    pm = order_matrix(False)

    def body(c):
        def order(i, v):
            v["x"] = nn(pm, tok[rows(4 * c + i, 128), :])

        def norm(i, v):
            at = rows(4 * c + i, 128)
            x = v.pop("x")
            s.tokp[at, :] = x.astype(BF)
            xhat, _ = norm_rows(x, None)
            s.nm[at, :] = (xhat * gain_attn[...]).astype(BF)
        pipeline(range(4), (order, norm), (0, 1))
    loop(2, body)


def st_cot(s, cot):
    pm = order_matrix(False)

    def body(c):
        for i in range(4):
            at = rows(4 * c + i, 128)
            s.cotp[at, :] = nn(pm, cot[at, :]).astype(BF)
    loop(2, body)


def transpose_into(dst, src):
    for c in range(4):
        dst[:, c * 256:(c + 1) * 256] = jnp.transpose(src[c * 256:(c + 1) * 256, :], (1, 0))


def block_sums(x):
    y = jnp.sum(x.reshape(16, 8, x.shape[1]), axis=0)
    return y[0:4] + y[4:8]


def st_values(s, w):
    for m in range(4):
        x = s.nm[rows(m, 256), :]
        for t in range(2):
            s.v[rows(m, 256), t * 256:(t + 1) * 256] = nn(x, w[t, :, VO:VO + HALF]).astype(BF)


def st_query_key(s, w):
    def product(m, v):
        x = s.nm[rows(m, 256), :]
        v["x"] = [nn(x, w[t, :, 0:512]).astype(BF) for t in range(2)]

    def store(m, v):
        at = rows(m, 256)
        for t, out in enumerate(v.pop("x")):
            cs = slice(t * 256, (t + 1) * 256)
            qv, kv = out[:, 0:256].astype(F32), out[:, 256:512].astype(F32)
            s.q[at, cs] = (qv * (1.0 / math.sqrt(HD))).astype(BF)
            s.k[at, cs] = out[:, 256:512]
            for ref, val in ((s.qm, qv), (s.km, kv)):
                sums = jnp.concatenate([block_sums(val[:128]), block_sums(val[128:])], axis=0)
                ref[rows(m, 8), cs] = sums * (1.0 / BLK)
    pipeline(range(4), (product, store), (0, 1))


def st_sinkhorn(s, seg, halfway=None):
    row = jnp.broadcast_to(seg[...], (NB, NB))
    ri, ci = iota((NB, NB), 0), iota((NB, NB), 1)
    col = jnp.sum(jnp.where(ri == ci, row, 0), axis=1, keepdims=True)
    allow = ((row == col) & (ci <= ri)) | ((row == 0) & (col > 0))
    s.allow[...] = allow.astype(F32)
    parts = []
    for p in range(4):
        cs = slice(p * 128, (p + 1) * 128)
        parts.append(nt(stack_heads(s.qm[:, cs]), s.km[:, cs], precision=HI))
    x = jnp.concatenate(parts, axis=0) * (BLK / math.sqrt(HD))
    mask = jnp.concatenate([allow.astype(F32)] * 8, axis=0) > 0
    x = jnp.where(mask, x, -1000000000.0)
    for it in range(ITERS):
        m = jnp.max(x, axis=1, keepdims=True)
        e = jnp.exp(x - m)
        z = jnp.sum(e, axis=1, keepdims=True)
        s.sk[2 * it] = e * (1.0 / z)
        x = x - (m + jnp.log(z))
        y = x.reshape(8, NB, NB)
        m = jnp.max(y, axis=1, keepdims=True)
        e = jnp.exp(y - m)
        z = jnp.sum(e, axis=1, keepdims=True)
        s.sk[2 * it + 1] = (e * (1.0 / z)).reshape(8 * NB, NB)
        x = (y - (m + jnp.log(z))).reshape(8 * NB, NB)
        if it == ITERS // 2 - 1 and halfway is not None:
            halfway()
    sorter = s.sk[2 * ITERS - 1].astype(BF)
    n = iota((128, NB), 0)
    e_mat = (((n >> 4) * 4 + (n & 3)) == iota((128, NB), 1)).astype(BF)
    wide = nt(sorter, e_mat).astype(BF)
    a, b = iota((128, 128), 0), iota((128, 128), 1)
    same = ((a >> 2) & 3) == ((b >> 2) & 3)
    for h in range(8):
        kr = jnp.where(same, nn(e_mat, wide[h * NB:(h + 1) * NB]), 0.0)
        s.kr[h] = kr.astype(BF)
        s.krt[h] = jnp.transpose(kr, (1, 0)).astype(BF)


def gather_chunk(ref, rq, cs):
    return jnp.concatenate([ref[pl.ds(pl.multiple_of(i * 128 + rq * 16, 16), 16), cs] for i in range(8)], axis=0)


def split_pair(x):
    return stack_heads(x)


def st_sort(s):
    def body(r):
        def mix(unit, v):
            rq, p = 2 * r + unit // 4, unit % 4
            cs = slice(p * 128, (p + 1) * 128)
            kv = jnp.concatenate([gather_chunk(s.k, rq, cs), gather_chunk(s.v, rq, cs)], axis=1)
            lhs = jnp.concatenate([s.kr[2 * p], s.kr[2 * p + 1]], axis=1)
            v["out"] = nn(lhs, split_pair(kv))

        def store(unit, v):
            rq, p = 2 * r + unit // 4, unit % 4
            cs = slice(p * 128, (p + 1) * 128)
            out = v.pop("out").astype(BF)
            for i in range(8):
                at = pl.ds(pl.multiple_of(i * 128 + rq * 16, 16), 16)
                s.ks[at, cs] = out[i * 16:(i + 1) * 16, 0:128]
                s.vs[at, cs] = out[i * 16:(i + 1) * 16, 128:256]
        pipeline(range(8), (mix, store), (0, 2))
    loop(4, body)


def st_bias(s):
    n, a = iota((256, 128), 0), iota((256, 128), 1)
    s.hidq[...] = ((a == (n & 3)) | (a == 4 + ((n & 127) >> 2))).astype(BF)
    other = (a < 4) & (a != (n & 3))
    later = (n < 128) & (a >= 4) & (a < 36) & ((n >> 2) > a - 4)
    s.hidk[...] = jnp.where(other | later, -1e30, 0.0).astype(BF)


def pick_rows(r):
    n = r.shape[1] // 2
    return jnp.concatenate([r[:64, :n], r[64:, n:]], axis=0)


def chunk_pair(c, i):
    p = i % 4
    c = c + i // 4
    return c, p, rows(c, 128), slice(p * 128, (p + 1) * 128)


def st_attend(s, b):
    def score(i, v):
        c, p, at, cs = chunk_pair(4 * b, i)
        qs = jnp.concatenate([stack_heads(s.q[at, cs]), s.hidq[...]], axis=1)
        kk = jnp.concatenate([jnp.concatenate([s.k[at, cs], s.ks[at, cs]], axis=0), s.hidk[...]], axis=1)
        v["x"] = nt(kk, qs)

    def soften(i, v):
        c, p, at, cs = chunk_pair(4 * b, i)
        x = v.pop("x")
        e = jnp.exp(x - jnp.max(x, axis=0, keepdims=True))
        v["p"] = (e * (1.0 / jnp.sum(e, axis=0, keepdims=True))).astype(BF)
        s.pr[p, c] = v["p"]

    def blend(i, v):
        c, p, at, cs = chunk_pair(4 * b, i)
        vv = jnp.concatenate([s.v[at, cs], s.vs[at, cs]], axis=0)
        v["o"] = pick_rows(nn(jnp.transpose(vv, (1, 0)), v.pop("p")))

    def store(i, v):
        c, p, at, cs = chunk_pair(4 * b, i)
        s.mix[at, cs] = jnp.transpose(v.pop("o"), (1, 0)).astype(BF)
    pipeline(range(16), (score, soften, blend, store), (0, 2, 4, 6))


def st_out(s, w, gain_ffn):
    def product(m, v):
        at = rows(m, 256)
        v["x"] = sum(nt(s.mix[at, t * 256:(t + 1) * 256], w[t, :, OO:OO + HALF]) for t in range(2))

    def norm(m, v):
        at = rows(m, 256)
        mid = s.tokp[at, :].astype(F32) + v.pop("x")
        s.mid[at, :] = mid
        s.res[at, :] = mid
        s.gnf[at, :] = jnp.zeros((256, D), F32)
        xhat, _ = norm_rows(mid, None)
        s.nf[at, :] = (xhat * gain_ffn[...]).astype(BF)
    pipeline(range(4), (product, norm), (0, 1))


def gelu_pair(x):
    k0, k1 = math.sqrt(2.0 / math.pi), 0.044715
    x2 = x * x
    half = 0.5 + 0.5 * jnp.tanh(x * (k0 + (k0 * k1) * x2))
    val = x * half
    der = half + (val - val * half) * (2 * k0 + (6 * k0 * k1) * x2)
    return val, der


def add_grads(g, other, t, own, cols, val):
    if own:
        val = val + other[:, :, :, cols].reshape(D, val.shape[1]).astype(F32)
    g[t, :, :, :, cols] = val.astype(BF).reshape(4, 4, D // 16, val.shape[1])


def st_ffn(s, w, t, u, out):
    ic, dc = span(FO + 2 * u * UNITS, UNITS), span(FO + (2 * u + 1) * UNITS, UNITS)

    def into(m, v):
        at = rows(m, 256)
        v["x"] = nn(s.nf[at, :], w[t, :, ic])
        v["g"] = nn(s.cotp[at, :], w[t, :, dc])

    def bend(m, v):
        at = rows(m, 256)
        val, der = gelu_pair(v.pop("x"))
        v["h"] = val.astype(BF)
        v["g"] = (v["g"] * der).astype(BF)
        s.hid[at, :] = v["h"]
        s.gp[at, :] = v["g"]

    def back(m, v):
        at = rows(m, 256)
        add = nt(v.pop("h"), w[t, :, dc])
        add = s.res[at, :] + add
        s.res[at, :] = add
        if out is not None:
            out[at, :] = add.astype(BF)
        add = nt(v.pop("g"), w[t, :, ic])
        s.gnf[at, :] = s.gnf[at, :] + add
    pipeline(range(4), (into, bend, back), (0, 2, 3))


def st_ffn_grads(s, g, other, t, u, own):
    add_grads(g, other, t, own, span(FO + 2 * u * UNITS, UNITS), nn(s.nft[...], s.gp[...]))
    add_grads(g, other, t, own, span(FO + (2 * u + 1) * UNITS, UNITS), nn(s.cott[...], s.hid[...]))


def st_mid_back(s, w, gain_ffn):
    parts = []

    def norm(m, v):
        at = rows(m, 256)
        xhat, inv = norm_rows(s.mid[at, :], None)
        gnf = s.gnf[at, :]
        parts.append(jnp.sum((gnf * xhat).reshape(32, 8, D), axis=0))
        gm = s.cotp[at, :].astype(F32) + norm_back(xhat, inv, gain_ffn[...], gnf)
        s.mid[at, :] = gm
        v["ga"] = gm.astype(BF)
        s.ga[at, :] = v["ga"]

    def product(m, v):
        at = rows(m, 256)
        ga = v.pop("ga")
        for t in range(2):
            s.gmix[at, t * 256:(t + 1) * 256] = nn(ga, w[t, :, OO:OO + HALF]).astype(BF)
        s.gat[:, m * 256:(m + 1) * 256] = jnp.transpose(ga, (1, 0))
    pipeline(range(4), (norm, product), (0, 1))
    s.gg[1:2, :] = jnp.sum(sum(parts), axis=0, keepdims=True)


def half_cols(t):
    return pl.ds(pl.multiple_of(t * HALF, HALF), HALF)


def st_out_grads(s, g, other, t, own):
    add_grads(g, other, t, own, slice(OO, OO + HALF), nn(s.gat[...], s.mix[:, half_cols(t)]))


def st_restore(src):
    pm = order_matrix(True)
    for c in range(8):
        at = slice(c * 128, (c + 1) * 128)
        src[at, :] = nn(pm, src[at, :]).astype(BF)


def pair_cols(t, j):
    return pl.ds(pl.multiple_of(t * HALF + j * 128, 128), 128)


def st_attend_back(s, t, after=None):
    scale = 1.0 / math.sqrt(HD)

    def place(i):
        c, j = i // 2, i % 2
        return c, 2 * t + j, slice(c * 128, (c + 1) * 128), pair_cols(t, j)

    def grad_probs(i, v):
        c, p, at, cs = place(i)
        g = s.gmix[at, cs]
        go = (g.astype(F32) * s.mix[at, cs].astype(F32)).astype(BF)
        vv = jnp.concatenate([s.v[at, cs], s.vs[at, cs]], axis=0)
        v["dp"] = nt(jnp.concatenate([vv, jnp.full_like(vv, -1.0)], axis=1),
                     jnp.concatenate([stack_heads(g), stack_heads(go)], axis=1))

    def grad_scores(i, v):
        c, p, at, cs = place(i)
        v["ds"] = (s.pr[p, c].astype(F32) * v.pop("dp")).astype(BF)

    def products(i, v):
        c, p, at, cs = place(i)
        ds = v.pop("ds")
        dkk = nn(ds, stack_heads(s.q[at, cs]))
        dvv = nn(s.pr[p, c], stack_heads(s.gmix[at, cs]))
        s.dk[at, cs] = dkk[:128]
        s.dks[at, cs] = dkk[128:].astype(BF)
        s.dv[at, cs] = dvv[:128]
        s.dvs[at, cs] = dvv[128:].astype(BF)
        kk = jnp.concatenate([s.k[at, cs], s.ks[at, cs]], axis=0)
        v["dq"] = pick_rows(nn(jnp.transpose(kk, (1, 0)), ds))

    def store(i, v):
        c, p, at, cs = place(i)
        s.dq[at, cs] = jnp.transpose(v.pop("dq"), (1, 0)) * scale
    pipeline(range(16), (grad_probs, grad_scores, products, store), (0, 2, 4, 6), after)


def st_sort_back(s, t):
    a, b = iota((128, 128), 0), iota((128, 128), 1)
    same = ((a >> 2) & 3) == ((b >> 2) & 3)
    accs = [[], []]

    def mix(i, v):
        j, rq = i // 8, i % 8
        cs = pair_cols(t, j)
        kv = jnp.concatenate([gather_chunk(s.k, rq, cs), gather_chunk(s.v, rq, cs)], axis=1)
        st = split_pair(jnp.concatenate([gather_chunk(s.dks, rq, cs), gather_chunk(s.dvs, rq, cs)], axis=1))
        accs[j].append(nt(st, kv))
        h = 4 * t + 2 * j
        v["out"] = nn(jnp.concatenate([s.krt[h], s.krt[h + 1]], axis=1), st)

    def store(i, v):
        j, rq = i // 8, i % 8
        cs = pair_cols(t, j)
        out = v.pop("out")
        for n in range(8):
            at = slice(n * 128 + rq * 16, n * 128 + rq * 16 + 16)
            s.dk[at, cs] = s.dk[at, cs] + out[n * 16:(n + 1) * 16, 0:128]
            s.dvb[at, cs] = (s.dv[at, cs] + out[n * 16:(n + 1) * 16, 128:256]).astype(BF)
    pipeline(range(16), (mix, store), (0, 2))
    x = jnp.concatenate([sum(accs[0]), sum(accs[1])], axis=0)
    x = jnp.where(jnp.concatenate([same] * 4, axis=0), x, 0.0)
    n = iota((128, NB), 0)
    cols_of = (((n >> 4) * 4 + (n & 3)) == iota((128, NB), 1)).astype(BF)
    m, n = iota((4 * NB, 512), 0), iota((4 * NB, 512), 1)
    rows_of = ((m >> 5) == (n >> 7)) & ((m & 31) == ((n >> 4) & 7) * 4 + (n & 3))
    high, low = two_terms(x)
    high, low = two_terms(nn(high, cols_of) + nn(low, cols_of))
    rows_of = rows_of.astype(BF)
    s.ds[pl.ds(pl.multiple_of(t * 4 * NB, 4 * NB), 4 * NB), :] = nn(rows_of, high) + nn(rows_of, low)


def two_terms(x):
    high = x.astype(BF)
    return high, (x - high.astype(F32)).astype(BF)


def sinkhorn_back(s, t):
    hs = pl.ds(pl.multiple_of(t * 4 * NB, 4 * NB), 4 * NB)
    v = {}

    def sweep(it):
        x = v["x"] if it < ITERS - 1 else s.ds[hs, :] * s.sk[2 * ITERS - 1, hs, :]
        y = x.reshape(4, NB, NB)
        pk = s.sk[2 * it + 1, hs, :].reshape(4, NB, NB)
        x = (y - pk * jnp.sum(y, axis=1, keepdims=True)).reshape(4 * NB, NB)
        v["x"] = x - s.sk[2 * it, hs, :] * jnp.sum(x, axis=1, keepdims=True)

    def means():
        mask = jnp.concatenate([s.allow[...]] * 4, axis=0) > 0
        x = jnp.where(mask, v.pop("x"), 0.0) * (1.0 / math.sqrt(HD))
        for j in range(2):
            cs = pair_cols(t, j)
            x0, x1 = x[2 * j * NB:(2 * j + 1) * NB], x[(2 * j + 1) * NB:(2 * j + 2) * NB]
            ev = even_lanes((NB, 128))
            km, qm = s.km[:, cs], s.qm[:, cs]
            v[j] = (jnp.where(ev, nn(x0, km, precision=HI), nn(x1, km, precision=HI)),
                    jnp.where(ev, tn(x0, qm, precision=HI), tn(x1, qm, precision=HI)))

    def spread(j):
        cs = pair_cols(t, j)
        dqm, dkm = v.pop(j)
        for c in range(8):
            at = slice(c * 128, (c + 1) * 128)
            for src, ref, dst in ((dqm, s.dq, s.dqb), (dkm, s.dk, s.dkb)):
                four = src[c * 4:(c + 1) * 4]
                eight = jnp.concatenate([four, four], axis=0)
                val = ref[at, cs].reshape(16, 8, 128) + eight[None]
                dst[at, cs] = val.reshape(128, 128).astype(BF)
    steps = [functools.partial(sweep, it) for it in reversed(range(ITERS))]
    return steps + [means, functools.partial(spread, 0), functools.partial(spread, 1)]


def st_value_grads(s, g, other, t, own):
    add_grads(g, other, t, own, slice(VO, VO + HALF), nn(s.nmt[...], s.dvb[:, half_cols(t)]))


def st_query_key_grads(s, g, other, t, own):
    for off, ref in ((QO, s.dqb), (KO, s.dkb)):
        add_grads(g, other, t, own, slice(off, off + HALF), nn(s.nmt[...], ref[:, half_cols(t)]))


def st_tokens_back(s, w, gain_attn, out):
    parts = []

    def product(m, v):
        at = rows(m, 256)
        v["g"] = 0.0
        for t in range(2):
            cs = slice(t * 256, (t + 1) * 256)
            v["g"] = v["g"] + nt(jnp.concatenate([s.dqb[at, cs], s.dkb[at, cs], s.dvb[at, cs]], axis=1), w[t, :, 0:768])

    def norm(m, v):
        at = rows(m, 256)
        gn = v.pop("g")
        xhat, inv = norm_rows(s.tokp[at, :].astype(F32), None)
        parts.append(jnp.sum((gn * xhat).reshape(32, 8, D), axis=0))
        out[at, :] = (s.mid[at, :] + norm_back(xhat, inv, gain_attn[...], gn)).astype(BF)
    pipeline(range(4), (product, norm), (0, 1))
    s.gg[0:1, :] = jnp.sum(sum(parts), axis=0, keepdims=True)


def attention_backward(s, w, g, other, c, gain_attn, out, hooks):
    st_attend_back(s, 1 - c)
    hooks["attend0"]()
    st_sort_back(s, 1 - c)
    steps = sinkhorn_back(s, 1 - c)

    st_attend_back(s, c, lambda n: steps[n]() if n < len(steps) else None)
    st_value_grads(s, g, None, 1 - c, False)
    st_query_key_grads(s, g, None, 1 - c, False)
    hooks["first"]()
    st_sort_back(s, c)
    hooks["sort1"]()
    st_value_grads(s, g, other, c, other is not None)
    hooks["values"]()
    for step in sinkhorn_back(s, c):
        step()
    st_query_key_grads(s, g, other, c, other is not None)
    hooks["last"]()
    st_tokens_back(s, w, gain_attn, out)


class Names:
    pass


def stage_names(refs):
    s = Names()
    for n, r in zip(SCRATCH, refs):
        setattr(s, n, r)
    for n, o in SHARED.items():
        setattr(s, n, getattr(s, o))
    return s


def layer_kernel(tok, cot, gain_attn, gain_ffn, w, seg, result, gtok, g, gg, *scr):
    s = stage_names(scr)
    st_tokens(s, tok, gain_attn)
    st_cot(s, cot)
    transpose_into(s.cott, s.cotp)
    transpose_into(s.nmt, s.nm)
    st_bias(s)
    st_query_key(s, w)
    st_sinkhorn(s, seg)
    st_values(s, w)
    st_sort(s)
    loop(2, functools.partial(st_attend, s))
    st_out(s, w, gain_ffn)
    transpose_into(s.nft, s.nf)
    def ffn(u):
        for t in range(2):
            st_ffn(s, w, t, u, result if t == 1 else None)
            st_ffn_grads(s, g, None, t, u, False)
    loop(2, ffn)
    st_mid_back(s, w, gain_ffn)
    for t in range(2):
        st_out_grads(s, g, None, t, False)
    attention_backward(s, w, g, None, 0, gain_attn, gtok, collections.defaultdict(lambda: lambda: None))
    st_restore(result)
    st_restore(gtok)
    gg[...] = s.gg[...]


def layer_call():
    vm = pl.BlockSpec(memory_space=pltpu.VMEM)
    return pl.pallas_call(
        layer_kernel,
        out_shape=(jax.ShapeDtypeStruct((T, D), BF), jax.ShapeDtypeStruct((T, D), BF),
                   jax.ShapeDtypeStruct((2, 4, 4, D // 16, COLS), BF), jax.ShapeDtypeStruct((8, D), F32)),
        in_specs=[vm] * 6, out_specs=(vm,) * 4,
        scratch_shapes=[pltpu.VMEM(*v) for v in SCRATCH.values()],
        compiler_params=pltpu.CompilerParams(vmem_limit_bytes=60 << 20),
    )


def last_kernel(res, gtok, grads, gains, result, grad_tokens, gain_a, gain_f, gq, gk, gv, go, gi, gd, hold, sems):
    parts = [(n, half) for half in range(res.shape[0]) for n in range(2)]
    ins = [pltpu.make_async_copy((res, gtok)[n].at[half], hold.at[n, half], sems.at[0, n, half]) for n, half in parts]
    outs = [pltpu.make_async_copy(hold.at[n, half], (result, grad_tokens)[n].at[half], sems.at[1, n, half]) for n, half in parts]
    for cp in ins:
        cp.start()
    width = gain_a.shape[1]
    gain_a[...] = gains[0:1, 0:width]
    gain_f[...] = gains[1:2, 0:width]
    for ref, val in zip((gq, gk, gv, go, gi, gd), split_cols(grads[...])):
        ref[...] = val
    for cp, out in zip(ins, outs):
        cp.wait()
        out.start()
    for out in outs:
        out.wait()


def last_call(res, gtok, grads, gains, width):
    vm, hbm = pl.BlockSpec(memory_space=pltpu.VMEM), pl.BlockSpec(memory_space=pl.ANY)
    square, long, row = (grads.shape[0], HALF), (grads.shape[0], FF // 2), (1, width)
    outs = [row, row, square, square, square, square, long, long]
    return pl.pallas_call(
        last_kernel,
        out_shape=(jax.ShapeDtypeStruct(res.shape, BF),) * 2 + tuple(jax.ShapeDtypeStruct(x, F32) for x in outs),
        in_specs=[hbm, hbm, vm, vm],
        out_specs=(hbm, hbm) + (vm,) * len(outs),
        scratch_shapes=[pltpu.VMEM((2,) + res.shape, BF), pltpu.SemaphoreType.DMA((2, 2, res.shape[0]))],
    )(res, gtok, grads, gains)


def split_cols(x):
    ins = jnp.concatenate([x[:, in_cols(u)] for u in range(2)], axis=1)
    downs = jnp.concatenate([x[:, down_cols(u)] for u in range(2)], axis=1)
    return x[:, QO:KO], x[:, KO:VO], x[:, VO:OO], x[:, OO:FO], ins, downs


def join_cols(q, k, v, o, i, d):
    parts = [q, k, v, o]
    for u in range(2):
        parts += [i[:, u * UNITS:(u + 1) * UNITS], d[:, u * UNITS:(u + 1) * UNITS]]
    return jnp.concatenate(parts, axis=1)


def by_collectives(tokens, gain_attn, gain_ffn, w_query, w_key, w_value, w_out, w_in, w_down, segment_ids, cotangent):
    tp = lax.axis_index("tp")
    tok = lax.all_to_all(tokens, "tp", 0, 0, tiled=True).reshape(T, D)
    cot = lax.all_to_all(cotangent, "tp", 0, 0, tiled=True).reshape(T, D)
    own = join_cols(w_query, w_key, w_value, w_out.T, w_in, w_down.T)
    half = lax.all_gather(own, "fsdp", axis=0, tiled=True)
    w = lax.all_gather(half, "tp", axis=0)
    seg = lax.dynamic_index_in_dim(segment_ids, tp, 0)
    res, gtok, g, gg = layer_call()(tok, cot, gain_attn[None], gain_ffn[None], w, seg)
    res = lax.all_to_all(res.reshape(tokens.shape), "tp", 0, 0, tiled=True)
    gtok = lax.all_to_all(gtok.reshape(tokens.shape), "tp", 0, 0, tiled=True)
    gsum = lax.psum_scatter(g.reshape(2, D, COLS).astype(F32), "tp", scatter_dimension=0)
    gsum = lax.psum_scatter(gsum, "fsdp", scatter_dimension=0, tiled=True)
    gains = lax.psum_scatter(gg, ("fsdp", "tp"), scatter_dimension=1, tiled=True)
    return finish(res, gtok, gsum, gains, gains.shape[1])


def finish(res, gtok, grads, gains, width):
    res, gtok, gain_a, gain_f, q, k, v, o, i, d = last_call(res, gtok, grads, gains, width)
    return res, gtok, gain_a.reshape(width), gain_f.reshape(width), q, k, v, o.T, i, d.T


PIECES = ((0, 512), (512, 1024), (1024, 2048), (2048, 3072))
GPIECES = ((1024, 2048), (2048, 3072), (768, 1024), (512, 768), (0, 512))
MESH = pl.DeviceIdType.MESH
ROWS = D // 16

EXCHANGE = dict(
    w=((2, D, COLS), BF), g=((2, 4, 4, ROWS, COLS), BF), other=((4, 4, ROWS, COLS), BF),
    rx=((3, 4, ROWS, COLS), BF), zs=((4, ROWS, COLS), BF), rz=((3, ROWS, COLS), BF),
    tok=((T, D), BF), cot=((T, D), BF), gr=((7, 8, D), F32), gs=((3, 8, D), F32),
)


def halves(lo, hi):
    mid = (lo + hi) // 2
    return slice(lo, mid), slice(mid, hi)


class Links:
    def __init__(self, e, sems):
        self.e = e
        self.sems = sems
        f, self.c = lax.axis_index("fsdp"), lax.axis_index("tp")
        self.zi, self.xy = f // 4, f % 4
        x, y = self.xy % 2, self.xy // 2
        self.f = f
        self.across = {"x": (1 - x) + 2 * y, "y": x + 2 * (1 - y), "d": (1 - x) + 2 * (1 - y)}
        self.arrival, self.sent = {}, []
        self.fixed = {}

    def z_at(self, dz):
        return (self.zi + dz) % 4

    def z_from(self, dz):
        return (self.zi + 4 - dz) % 4

    def greet(self):
        self.bar = pltpu.get_barrier_semaphore()
        for dev in ([(self.z_at(d) * 4 + self.xy, self.c) for d in (1, 2, 3)]
                    + [(self.zi * 4 + k, self.c) for k in self.across.values()] + [(self.f, 1 - self.c)]):
            pl.semaphore_signal(self.bar, inc=1, device_id=dev, device_id_type=MESH)

    def meet(self):
        pl.semaphore_wait(self.bar, 7)

    def w_rows(self, first, count, cols):
        return self.e.w.at[self.c, pl.ds(pl.multiple_of(first * ROWS, count * ROWS), count * ROWS), cols]

    def mine(self, k, cols):
        return self.e.g.at[self.c, :, self.across[k], :, cols]

    def route(self, kind, *key):
        e = self.e
        if kind in self.fixed:
            return self.fixed[kind][key[0]] + ("t",)
        if kind in ("z", "x", "y", "d", "xy", "yx", "t"):
            piece, d = key
            cols = slice(*PIECES[piece])
            first, second = halves(*PIECES[piece])
            if kind == "z":
                at, to = self.w_rows(self.f, 1, cols), d
            elif kind == "t":
                at, to = self.w_rows(self.z_from(d) * 4, 4, cols), "t"
            elif kind == "xy":
                at, to = self.w_rows(self.z_from(d) * 4 + self.across["x"], 1, first), "y"
            elif kind == "yx":
                at, to = self.w_rows(self.z_from(d) * 4 + self.across["y"], 1, second), "x"
            else:
                at, to = self.w_rows(self.z_from(d) * 4 + self.xy, 1, cols), kind
            return at, at, to
        if kind == "n":
            n = key[0]
            return e.gs.at[0 if n == 0 else 1 if n < 4 else 2], e.gr.at[n], "t" if n == 0 else "xyd"[n - 1] if n < 4 else n - 3
        piece = key[0]
        if kind == "gt":
            lo, hi = GPIECES[piece] if piece < 3 else (0, OO)
            return e.g.at[1 - self.c, :, :, :, lo:hi], e.other.at[:, :, :, lo:hi], "t"
        cols = slice(*GPIECES[piece])
        if kind == "gz":
            d = key[1]
            return e.zs.at[d, :, cols], e.rz.at[d - 1, :, cols], d
        to = kind[1]
        if len(key) > 1:
            cols = halves(*GPIECES[piece])[key[1]]
            if kind == "gd":
                to = "xy"[key[1]]
        return self.mine(kind[1], cols), e.rx.at["xyd".index(kind[1]), :, :, cols], to

    def copy(self, key):
        src, dst, to = self.route(*key)
        if isinstance(to, int):
            dev = (self.z_at(to) * 4 + self.xy, self.c)
        elif to == "t":
            dev = (self.f, 1 - self.c)
        else:
            dev = (self.zi * 4 + self.across[to], self.c)
        sent = self.sent.index(key) % NSEND if key in self.sent else 0
        return pltpu.make_async_remote_copy(
            src_ref=src, dst_ref=dst, send_sem=self.sems[0].at[sent],
            recv_sem=self.sems[1].at[self.arrival.setdefault(key, len(self.arrival))], device_id=dev, device_id_type=MESH)

    def send(self, *key):
        self.sent.append(key)
        if len(self.sent) > NSEND:
            self.copy(self.sent[-1 - NSEND]).wait_send()
        self.copy(key).start()

    def arrived(self, *key):
        self.copy(key).wait_recv()

    def finish(self):
        assert len(self.sent) == len(self.arrival) == NSEM, len(self.sent)
        for key in self.sent[-NSEND:]:
            self.copy(key).wait_send()

    def own_z(self, piece):
        for d in (1, 2, 3):
            self.send("z", piece, d)

    def own_plane(self, piece):
        self.to_plane(piece, 0)

    def to_plane(self, piece, d):
        for k in "xyd" if piece < 2 else "xy":
            self.send(k, piece, d)

    def plane(self, piece, d):
        self.arrived("z", piece, d)
        self.to_plane(piece, d)

    def corner(self, piece, d):
        self.arrived("x", piece, d)
        self.send("xy", piece, d)
        self.arrived("y", piece, d)
        self.send("yx", piece, d)

    def pair(self, piece, d):
        for k in ("x", "y", "d") if piece < 2 else ("xy", "yx"):
            self.arrived(k, piece, d)
        self.send("t", piece, d)

    def gathered(self, piece):
        for d in range(4):
            self.arrived("t", piece, d)

    def grads_pair(self, piece):
        self.send("gt", piece)

    def grads_plane(self, piece):
        for k in "xyd":
            self.send("g" + k, piece)

    def grads_part(self, piece):
        self.send("gd", piece, 0)
        self.send("gd", piece, 1)
        self.send("gx", piece, 0)
        self.send("gy", piece, 1)

    def grads_join(self, piece):
        first, second = halves(*GPIECES[piece])
        for n, k, cols in ((0, "y", first), (1, "x", second)):
            self.arrived("gd", piece, n)
            at = self.mine(k, cols)
            at[...] = (at[...].astype(F32) + self.e.rx[2, :, :, cols].astype(F32)).astype(BF)
            self.send("g" + k, piece, n)

    def grads_line(self, piece, direct):
        e = self.e
        cols = slice(*GPIECES[piece])
        if direct:
            for k in "xyd":
                self.arrived("g" + k, piece)
        else:
            for k in "xy":
                for n in range(2):
                    self.arrived("g" + k, piece, n)
        for d in (1, 2, 3, 0):
            z = self.z_at(d)
            total = e.g[self.c, z, self.xy, :, cols].astype(F32)
            for n in range(3 if direct else 2):
                total = total + e.rx[n, z, :, cols].astype(F32)
            if d:
                e.zs[d, :, cols] = total.astype(BF)
                self.send("gz", piece, d)
            else:
                self.out[:, cols] = total

    def grads_in(self, piece):
        cols = slice(*GPIECES[piece])
        for d in (1, 2, 3):
            self.arrived("gz", piece, d)
        total = self.out[:, cols]
        for d in range(3):
            total = total + self.e.rz[d, :, cols].astype(F32)
        self.out[:, cols] = total

    def gains_sum(self, step):
        e = self.e
        if step == 0:
            self.send("n", 0)
        if step == 1:
            self.arrived("n", 0)
            e.gs[1] = e.gs[0] + e.gr[0]
            for n in (1, 2, 3):
                self.send("n", n)
        if step == 2:
            for n in (1, 2, 3):
                self.arrived("n", n)
            e.gs[2] = e.gs[1] + e.gr[1] + e.gr[2] + e.gr[3]
            for n in (4, 5, 6):
                self.send("n", n)
        if step == 3:
            for n in (4, 5, 6):
                self.arrived("n", n)
            return e.gs[2] + e.gr[4] + e.gr[5] + e.gr[6]


NSEM = 135
NSEND = 24


def step_kernel(tokens, cotangent, gain_attn, gain_ffn, wq, wk, wv, wo, wi, wd, seg, result, gtok, gout, gains, *scr):
    ns, ne = len(SCRATCH), len(EXCHANGE)
    s = stage_names(scr[:ns])
    e = Names()
    for n, r in zip(EXCHANGE, scr[ns:ns + ne]):
        setattr(e, n, r)
    send_sem, recv_sem, local = scr[ns + ne:]
    link = Links(e, (send_sem, recv_sem))
    link.out = gout
    c, f, w, g = link.c, link.f, e.w, e.g
    half = T // 2
    mine = pl.ds(pl.multiple_of(c * half, half), half)
    theirs = pl.ds(pl.multiple_of((1 - c) * half, half), half)
    four, three = range(4), (1, 2, 3)

    link.fixed = {"in": [(tokens.at[1 - c], e.tok.at[mine, :]), (cotangent.at[1 - c], e.cot.at[mine, :])],
                  "out": [(e.cot.at[theirs, :], gtok.at[c]), (e.tok.at[theirs, :], result.at[c])]}
    loads = [pltpu.make_async_copy(tokens.at[c], e.tok.at[mine, :], local.at[0]),
             pltpu.make_async_copy(cotangent.at[c], e.cot.at[mine, :], local.at[1])]
    for cp in loads:
        cp.start()
    link.greet()
    w[c, pl.ds(pl.multiple_of(f * ROWS, ROWS), ROWS), :] = join_cols(wq[...], wk[...], wv[...], wo[...], wi[...], wd[...])
    link.meet()
    link.own_z(0)
    link.own_plane(0)
    link.send("in", 0)
    link.send("in", 1)
    link.own_z(1)
    link.own_plane(1)
    link.own_plane(2)
    loads[0].wait()
    link.arrived("in", 0)
    st_tokens(s, e.tok, gain_attn)
    loads[1].wait()
    link.arrived("in", 1)
    st_cot(s, e.cot)
    transpose_into(s.nmt, s.nm)
    for d in three:
        link.plane(0, d)
    link.own_z(2)
    transpose_into(s.cott, s.cotp)
    st_bias(s)
    for d in three:
        link.plane(1, d)
    for d in four:
        link.pair(0, d)
    link.own_z(3)
    link.gathered(0)
    st_query_key(s, w)
    link.plane(2, 1)
    link.plane(2, 2)

    def halfway():
        for d in four:
            link.pair(1, d)
        link.plane(2, 3)
        link.own_plane(3)
    st_sinkhorn(s, seg.at[pl.ds(c, 1), :], halfway)
    link.gathered(1)
    st_values(s, w)
    link.corner(2, 0)
    link.corner(2, 1)
    st_sort(s)
    link.plane(3, 1)
    link.corner(2, 2)
    link.corner(2, 3)
    st_attend(s, 0)
    link.plane(3, 2)
    link.plane(3, 3)
    link.pair(2, 0)
    link.pair(2, 1)
    st_attend(s, 1)
    link.pair(2, 2)
    link.pair(2, 3)
    link.corner(3, 0)
    link.corner(3, 1)
    st_out(s, w, gain_ffn)
    transpose_into(s.nft, s.nf)
    link.gathered(2)

    def ffn(u):
        early, late = u == 0, u == 1
        pl.when(late)(lambda: link.gathered(3))
        st_ffn(s, w, 1 - c, u, None)

        @pl.when(early)
        def _():
            link.corner(3, 2)
            link.corner(3, 3)
            link.pair(3, 0)
            link.pair(3, 1)
        st_ffn_grads(s, g, None, 1 - c, u, False)
        for n in range(2):
            pl.when(u == n)(functools.partial(link.grads_pair, n))
        st_ffn(s, w, c, u, e.tok)

        @pl.when(early)
        def _():
            link.pair(3, 2)
            link.pair(3, 3)
            link.arrived("gt", 0)

        @pl.when(late)
        def _():
            link.grads_join(0)
            link.arrived("gt", 1)
        st_ffn_grads(s, g, e.other, c, u, True)
        for n in range(2):
            pl.when(u == n)(functools.partial(link.grads_part, n))
    loop(2, ffn)
    st_mid_back(s, w, gain_ffn)
    st_out_grads(s, g, None, 1 - c, False)
    link.grads_pair(2)
    link.grads_line(0, False)
    link.arrived("gt", 2)
    st_out_grads(s, g, e.other, c, True)
    link.grads_plane(2)

    def attend0():
        link.grads_join(1)

    def first():
        link.grads_pair(3)
        link.grads_in(0)

    def sort1():
        link.arrived("gt", 3)
        link.grads_line(1, False)

    def values():
        link.grads_plane(3)
        link.grads_line(2, True)

    def last():
        link.grads_plane(4)

    attention_backward(s, w, g, e.other, c, gain_attn, e.cot, {
        "attend0": attend0, "first": first, "sort1": sort1, "values": values, "last": last})
    e.gs[0] = s.gg[...]
    link.gains_sum(0)
    stores = []
    for n, (buf, out) in enumerate(((e.cot, gtok), (e.tok, result))):
        st_restore(buf)
        stores.append(pltpu.make_async_copy(buf.at[mine, :], out.at[c], local.at[2 + n]))
        stores[n].start()
        link.send("out", n)
    link.grads_line(3, True)
    link.gains_sum(1)
    link.grads_in(1)
    link.grads_in(2)
    link.grads_line(4, True)
    link.gains_sum(2)
    link.grads_in(3)
    link.arrived("out", 0)
    link.arrived("out", 1)
    for cp in stores:
        cp.wait()
    total = link.gains_sum(3)
    width = D // 32
    pick = (iota((D, 128), 0) == iota((D, 128), 1) + (2 * f + c) * width).astype(F32)
    gains[...] = nn(total, pick, precision=HI)
    link.grads_in(4)
    link.finish()


def by_kernel(tokens, gain_attn, gain_ffn, w_query, w_key, w_value, w_out, w_in, w_down, segment_ids, cotangent):
    vm, hbm = pl.BlockSpec(memory_space=pltpu.VMEM), pl.BlockSpec(memory_space=pl.ANY)
    shapes = list(SCRATCH.values()) + list(EXCHANGE.values())
    res, gtok, grads, gains = pl.pallas_call(
        step_kernel,
        out_shape=(jax.ShapeDtypeStruct(tokens.shape, BF), jax.ShapeDtypeStruct(tokens.shape, BF),
                   jax.ShapeDtypeStruct((ROWS, COLS), F32), jax.ShapeDtypeStruct((8, 128), F32)),
        in_specs=[hbm] * 2 + [vm] * 9, out_specs=(hbm, hbm, vm, vm),
        scratch_shapes=[pltpu.VMEM(*v) for v in shapes] + [
            pltpu.SemaphoreType.DMA((NSEND,)), pltpu.SemaphoreType.DMA((NSEM,)), pltpu.SemaphoreType.DMA((4,))],
        compiler_params=pltpu.CompilerParams(collective_id=0, has_side_effects=True, vmem_limit_bytes=63 << 20),
    )(tokens, cotangent, gain_attn[None], gain_ffn[None], w_query, w_key, w_value, w_out.T, w_in, w_down.T, segment_ids)
    return finish(res, gtok, grads, gains, D // 32)


def solution(mesh):
    body = by_kernel if mesh.shape["fsdp"] == 16 else by_collectives
    return jax.shard_map(
        body,
        mesh=mesh,
        in_specs=(P(None, ("fsdp", "tp"), None), P(), P(), P("fsdp", "tp"), P("fsdp", "tp"), P("fsdp", "tp"),
                  P("tp", "fsdp"), P("fsdp", "tp"), P("tp", "fsdp"), P(None, "fsdp"), P(None, ("fsdp", "tp"), None)),
        out_specs=(P(None, ("fsdp", "tp"), None), P(None, ("fsdp", "tp"), None), P(("fsdp", "tp")), P(("fsdp", "tp")),
                   P("fsdp", "tp"), P("fsdp", "tp"), P("fsdp", "tp"), P("tp", "fsdp"), P("fsdp", "tp"), P("tp", "fsdp")),
        check_vma=False,
    )
```

profile of v0, /device:TPU:0, one launch (start us, length us, event | category | flops | bytes accessed | tf_op | source)
XLA Modules:
  0.0 91.7 jit_solution(17409826072327425597)
XLA Ops:
  0.6 86.7 %shard_map.186 = (bf16[2,512,512]{2,1,0:T(8,128)(2,1)}, bf16[2,512,512]{2,1,0:T(8,128)(2,1)}, f32[32,3072]{1,0:T(8,128)}, f32[8,128]{1,0:T(8,128)}) custom-call(bf16[2,512,512]{2,1,0:T(8,128)(2,1)} %tokens.1, bf16[2,512,512]{2,1,0:T(8,128)(2,1)} %cotangent.1, f32[1,512]{1,0:T(1,128)} %bitcast.10, f32[1,512]{1,0:T(1,128)} %bitcast.11, bf16[32,256]{1,0:T(8,128)(2,1)} %wq.1, ...), custom_call_target="tpu_custom_call" | custom-call | tf_op jit(solution)/shard_map/pallas_call | solution.py:1066
  87.3 4.2 %shard_map.187 = (bf16[2,512,512]{2,1,0:T(8,128)(2,1)}, bf16[2,512,512]{2,1,0:T(8,128)(2,1)}, f32[1,16]{1,0:T(1,128)}, f32[1,16]{1,0:T(1,128)}, f32[32,256]{1,0:...) custom-call(bf16[2,512,512]{2,1,0:T(8,128)(2,1)} %get-tuple-element., ...), custom_call_target="tpu_custom_call" | custom-call | tf_op jit(solution)/shard_map/pallas_call | solution.py:633
where the time goes:
time: 91.9 us; the launch traced here: 91.7 us
  Pallas kernels  90.9 us (99%)
    pallas_call x1, Pallas kernels, by_kernel(): pl.pallas_call(step_kernel, out_shape=(jax.ShapeDtypeStruct(tokens.shape,...  86.7 us
    pallas_call x1, Pallas kernels, last_call(): pl.pallas_call(last_kernel, out_shape=(jax.ShapeDtypeStruct(res.shape, BF...  4.17 us

commit v1 on v0

--- a/solution.py
+++ b/solution.py
@@ -12,8 +12,9 @@
 HD, BLK, ITERS, NB, D, FF, T = 64, 32, 8, 32, 512, 2048, 1024
 HALF = D // 2
 COLS = 3 * HALF + HALF + FF
-QO, KO, VO, OO, FO = 0, 256, 512, 768, 1024
+QO, VO, OO, FO = 0, 512, 768, 1024
 UNITS = 512
+STEPS = FF // 2 // UNITS
 
 
 def in_cols(u):
@@ -165,9 +166,11 @@
         at = rows(m, 256)
         for t, out in enumerate(v.pop("x")):
             cs = slice(t * 256, (t + 1) * 256)
-            qv, kv = out[:, 0:256].astype(F32), out[:, 256:512].astype(F32)
+            queries = jnp.concatenate([out[:, 0:128], out[:, 256:384]], axis=1)
+            keys = jnp.concatenate([out[:, 128:256], out[:, 384:512]], axis=1)
+            qv, kv = queries.astype(F32), keys.astype(F32)
             s.q[at, cs] = (qv * (1.0 / math.sqrt(HD))).astype(BF)
-            s.k[at, cs] = out[:, 256:512]
+            s.k[at, cs] = keys
             for ref, val in ((s.qm, qv), (s.km, kv)):
                 sums = jnp.concatenate([block_sums(val[:128]), block_sums(val[128:])], axis=0)
                 ref[rows(m, 8), cs] = sums * (1.0 / BLK)
@@ -392,11 +395,11 @@
     return pl.ds(pl.multiple_of(t * HALF + j * 128, 128), 128)
 
 
-def st_attend_back(s, t, after=None):
+def st_attend_back(s, t, pairs, after=None):
     scale = 1.0 / math.sqrt(HD)
 
     def place(i):
-        c, j = i // 2, i % 2
+        c, j = i // len(pairs), pairs[i % len(pairs)]
         return c, 2 * t + j, slice(c * 128, (c + 1) * 128), pair_cols(t, j)
 
     def grad_probs(i, v):
@@ -426,16 +429,21 @@
     def store(i, v):
         c, p, at, cs = place(i)
         s.dq[at, cs] = jnp.transpose(v.pop("dq"), (1, 0)) * scale
-    pipeline(range(16), (grad_probs, grad_scores, products, store), (0, 2, 4, 6), after)
-
-
-def st_sort_back(s, t):
+    pipeline(range(8 * len(pairs)), (grad_probs, grad_scores, products, store), (0, 2, 4, 6), after)
+
+
+def heads_at(t, pairs):
+    n = 2 * NB
+    return pl.ds(pl.multiple_of(t * 2 * n + pairs[0] * n, n), n * len(pairs))
+
+
+def st_sort_back(s, t, pairs):
     a, b = iota((128, 128), 0), iota((128, 128), 1)
     same = ((a >> 2) & 3) == ((b >> 2) & 3)
-    accs = [[], []]
+    accs = {j: [] for j in pairs}
 
     def mix(i, v):
-        j, rq = i // 8, i % 8
+        j, rq = pairs[i // 8], i % 8
         cs = pair_cols(t, j)
         kv = jnp.concatenate([gather_chunk(s.k, rq, cs), gather_chunk(s.v, rq, cs)], axis=1)
         st = split_pair(jnp.concatenate([gather_chunk(s.dks, rq, cs), gather_chunk(s.dvs, rq, cs)], axis=1))
@@ -444,24 +452,28 @@
         v["out"] = nn(jnp.concatenate([s.krt[h], s.krt[h + 1]], axis=1), st)
 
     def store(i, v):
-        j, rq = i // 8, i % 8
+        j, rq = pairs[i // 8], i % 8
         cs = pair_cols(t, j)
         out = v.pop("out")
         for n in range(8):
             at = slice(n * 128 + rq * 16, n * 128 + rq * 16 + 16)
             s.dk[at, cs] = s.dk[at, cs] + out[n * 16:(n + 1) * 16, 0:128]
             s.dvb[at, cs] = (s.dv[at, cs] + out[n * 16:(n + 1) * 16, 128:256]).astype(BF)
-    pipeline(range(16), (mix, store), (0, 2))
-    x = jnp.concatenate([sum(accs[0]), sum(accs[1])], axis=0)
-    x = jnp.where(jnp.concatenate([same] * 4, axis=0), x, 0.0)
-    n = iota((128, NB), 0)
-    cols_of = (((n >> 4) * 4 + (n & 3)) == iota((128, NB), 1)).astype(BF)
-    m, n = iota((4 * NB, 512), 0), iota((4 * NB, 512), 1)
-    rows_of = ((m >> 5) == (n >> 7)) & ((m & 31) == ((n >> 4) & 7) * 4 + (n & 3))
-    high, low = two_terms(x)
-    high, low = two_terms(nn(high, cols_of) + nn(low, cols_of))
-    rows_of = rows_of.astype(BF)
-    s.ds[pl.ds(pl.multiple_of(t * 4 * NB, 4 * NB), 4 * NB), :] = nn(rows_of, high) + nn(rows_of, low)
+    pipeline(range(8 * len(pairs)), (mix, store), (0, 2))
+
+    def fold():
+        heads = 2 * len(pairs)
+        x = jnp.concatenate([sum(accs[j]) for j in pairs], axis=0)
+        x = jnp.where(jnp.concatenate([same] * heads, axis=0), x, 0.0)
+        n = iota((128, NB), 0)
+        cols_of = (((n >> 4) * 4 + (n & 3)) == iota((128, NB), 1)).astype(BF)
+        m, n = iota((heads * NB, heads * 128), 0), iota((heads * NB, heads * 128), 1)
+        rows_of = ((m >> 5) == (n >> 7)) & ((m & 31) == ((n >> 4) & 7) * 4 + (n & 3))
+        high, low = two_terms(x)
+        high, low = two_terms(nn(high, cols_of) + nn(low, cols_of))
+        rows_of = rows_of.astype(BF)
+        s.ds[heads_at(t, pairs), :] = nn(rows_of, high) + nn(rows_of, low)
+    return fold
 
 
 def two_terms(x):
@@ -469,23 +481,23 @@
     return high, (x - high.astype(F32)).astype(BF)
 
 
-def sinkhorn_back(s, t):
-    hs = pl.ds(pl.multiple_of(t * 4 * NB, 4 * NB), 4 * NB)
+def sinkhorn_back(s, t, pairs):
+    hs, n = heads_at(t, pairs), 2 * len(pairs)
     v = {}
 
     def sweep(it):
         x = v["x"] if it < ITERS - 1 else s.ds[hs, :] * s.sk[2 * ITERS - 1, hs, :]
-        y = x.reshape(4, NB, NB)
-        pk = s.sk[2 * it + 1, hs, :].reshape(4, NB, NB)
-        x = (y - pk * jnp.sum(y, axis=1, keepdims=True)).reshape(4 * NB, NB)
+        y = x.reshape(n, NB, NB)
+        pk = s.sk[2 * it + 1, hs, :].reshape(n, NB, NB)
+        x = (y - pk * jnp.sum(y, axis=1, keepdims=True)).reshape(n * NB, NB)
         v["x"] = x - s.sk[2 * it, hs, :] * jnp.sum(x, axis=1, keepdims=True)
 
     def means():
-        mask = jnp.concatenate([s.allow[...]] * 4, axis=0) > 0
+        mask = jnp.concatenate([s.allow[...]] * n, axis=0) > 0
         x = jnp.where(mask, v.pop("x"), 0.0) * (1.0 / math.sqrt(HD))
-        for j in range(2):
+        for h, j in enumerate(pairs):
             cs = pair_cols(t, j)
-            x0, x1 = x[2 * j * NB:(2 * j + 1) * NB], x[(2 * j + 1) * NB:(2 * j + 2) * NB]
+            x0, x1 = x[2 * h * NB:(2 * h + 1) * NB], x[(2 * h + 1) * NB:(2 * h + 2) * NB]
             ev = even_lanes((NB, 128))
             km, qm = s.km[:, cs], s.qm[:, cs]
             v[j] = (jnp.where(ev, nn(x0, km, precision=HI), nn(x1, km, precision=HI)),
@@ -502,16 +514,21 @@
                 val = ref[at, cs].reshape(16, 8, 128) + eight[None]
                 dst[at, cs] = val.reshape(128, 128).astype(BF)
     steps = [functools.partial(sweep, it) for it in reversed(range(ITERS))]
-    return steps + [means, functools.partial(spread, 0), functools.partial(spread, 1)]
-
-
-def st_value_grads(s, g, other, t, own):
-    add_grads(g, other, t, own, slice(VO, VO + HALF), nn(s.nmt[...], s.dvb[:, half_cols(t)]))
-
-
-def st_query_key_grads(s, g, other, t, own):
-    for off, ref in ((QO, s.dqb), (KO, s.dkb)):
-        add_grads(g, other, t, own, slice(off, off + HALF), nn(s.nmt[...], ref[:, half_cols(t)]))
+    return steps + [means] + [functools.partial(spread, j) for j in pairs]
+
+
+def st_value_grads(s, g, other, t, own, part):
+    val = nn(s.nmt[part * 256:(part + 1) * 256, :], s.dvb[:, half_cols(t)])
+    if own:
+        val = val + other[2 * part:2 * part + 2, :, :, VO:OO].reshape(256, HALF).astype(F32)
+    g[t, 2 * part:2 * part + 2, :, :, VO:OO] = val.astype(BF).reshape(2, 4, D // 16, HALF)
+
+
+def st_query_key_grads(s, g, other, t, own, pairs):
+    for j in pairs:
+        cs = pair_cols(t, j)
+        add_grads(g, other, t, own, slice(j * 256, (j + 1) * 256),
+                  nn(s.nmt[...], jnp.concatenate([s.dqb[:, cs], s.dkb[:, cs]], axis=1)))
 
 
 def st_tokens_back(s, w, gain_attn, out):
@@ -522,7 +539,9 @@
         v["g"] = 0.0
         for t in range(2):
             cs = slice(t * 256, (t + 1) * 256)
-            v["g"] = v["g"] + nt(jnp.concatenate([s.dqb[at, cs], s.dkb[at, cs], s.dvb[at, cs]], axis=1), w[t, :, 0:768])
+            dq, dk = s.dqb[at, cs], s.dkb[at, cs]
+            lhs = jnp.concatenate([dq[:, :128], dk[:, :128], dq[:, 128:], dk[:, 128:], s.dvb[at, cs]], axis=1)
+            v["g"] = v["g"] + nt(lhs, w[t, :, 0:OO])
 
     def norm(m, v):
         at = rows(m, 256)
@@ -535,22 +554,32 @@
 
 
 def attention_backward(s, w, g, other, c, gain_attn, out, hooks):
-    st_attend_back(s, 1 - c)
+    own, both = other is not None, (0, 1)
+
+    def with_steps(steps):
+        return lambda n: steps[n]() if n < len(steps) else None
+    st_attend_back(s, 1 - c, both)
     hooks["attend0"]()
-    st_sort_back(s, 1 - c)
-    steps = sinkhorn_back(s, 1 - c)
-
-    st_attend_back(s, c, lambda n: steps[n]() if n < len(steps) else None)
-    st_value_grads(s, g, None, 1 - c, False)
-    st_query_key_grads(s, g, None, 1 - c, False)
+    fold = st_sort_back(s, 1 - c, both)
+    hooks["sort0"]()
+    st_attend_back(s, c, (0,), with_steps([fold] + sinkhorn_back(s, 1 - c, both)))
+    for part in range(2):
+        st_value_grads(s, g, None, 1 - c, False, part)
+    st_query_key_grads(s, g, None, 1 - c, False, both)
     hooks["first"]()
-    st_sort_back(s, c)
-    hooks["sort1"]()
-    st_value_grads(s, g, other, c, other is not None)
-    hooks["values"]()
-    for step in sinkhorn_back(s, c):
+    fold = st_sort_back(s, c, (0,))
+    st_attend_back(s, c, (1,), with_steps([fold] + sinkhorn_back(s, c, (0,))))
+    hooks["pair"]()
+    st_query_key_grads(s, g, other, c, own, (0,))
+    hooks["queries"]()
+    steps = [st_sort_back(s, c, (1,))] + sinkhorn_back(s, c, (1,))
+    for n, step in enumerate(steps):
         step()
-    st_query_key_grads(s, g, other, c, other is not None)
+        if n in (0, 2):
+            st_value_grads(s, g, other, c, own, n // 2)
+        if n == 3:
+            hooks["values"]()
+    st_query_key_grads(s, g, other, c, own, (1,))
     hooks["last"]()
     st_tokens_back(s, w, gain_attn, out)
 
@@ -608,22 +637,38 @@
     )
 
 
-def last_kernel(res, gtok, grads, gains, result, grad_tokens, gain_a, gain_f, gq, gk, gv, go, gi, gd, hold, sems):
-    parts = [(n, half) for half in range(res.shape[0]) for n in range(2)]
-    ins = [pltpu.make_async_copy((res, gtok)[n].at[half], hold.at[n, half], sems.at[0, n, half]) for n, half in parts]
-    outs = [pltpu.make_async_copy(hold.at[n, half], (result, grad_tokens)[n].at[half], sems.at[1, n, half]) for n, half in parts]
-    for cp in ins:
+def last_kernel(res, gtok, grads, gains, result, grad_tokens, gain_a, gain_f, gq, gk, gv, go, gi, gd, hold, held, sems):
+    sem = iter(range(sems.shape[0]))
+
+    def copy(src, dst):
+        return pltpu.make_async_copy(src, dst, sems.at[next(sem)])
+    moves = [(copy(grads, held), [copy(held.at[:, cols], ref.at[:, at]) for cols, ref, at in places(gq, gk, gv, go, gi, gd)])]
+    for half in range(res.shape[0]):
+        for n, (src, dst) in enumerate(((res, result), (gtok, grad_tokens))):
+            moves.append((copy(src.at[half], hold.at[n, half]), [copy(hold.at[n, half], dst.at[half])]))
+    for cp, _ in moves:
         cp.start()
     width = gain_a.shape[1]
     gain_a[...] = gains[0:1, 0:width]
     gain_f[...] = gains[1:2, 0:width]
-    for ref, val in zip((gq, gk, gv, go, gi, gd), split_cols(grads[...])):
-        ref[...] = val
-    for cp, out in zip(ins, outs):
+    for cp, outs in moves:
         cp.wait()
-        out.start()
-    for out in outs:
-        out.wait()
+        for out in outs:
+            out.start()
+    for _, outs in moves:
+        for out in outs:
+            out.wait()
+
+
+def places(gq, gk, gv, go, gi, gd):
+    runs = [(slice(VO, OO), gv, slice(0, HALF)), (slice(OO, FO), go, slice(0, HALF))]
+    for j in range(2):
+        at = slice(j * 128, (j + 1) * 128)
+        runs += [(slice(j * 256, j * 256 + 128), gq, at), (slice(j * 256 + 128, (j + 1) * 256), gk, at)]
+    for u in range(STEPS):
+        at = slice(u * UNITS, (u + 1) * UNITS)
+        runs += [(in_cols(u), gi, at), (down_cols(u), gd, at)]
+    return runs
 
 
 def last_call(res, gtok, grads, gains, width):
@@ -633,21 +678,19 @@
     return pl.pallas_call(
         last_kernel,
         out_shape=(jax.ShapeDtypeStruct(res.shape, BF),) * 2 + tuple(jax.ShapeDtypeStruct(x, F32) for x in outs),
-        in_specs=[hbm, hbm, vm, vm],
-        out_specs=(hbm, hbm) + (vm,) * len(outs),
-        scratch_shapes=[pltpu.VMEM((2,) + res.shape, BF), pltpu.SemaphoreType.DMA((2, 2, res.shape[0]))],
+        in_specs=[hbm, hbm, hbm, vm],
+        out_specs=(hbm, hbm, vm, vm) + (hbm,) * 6,
+        scratch_shapes=[pltpu.VMEM((2,) + res.shape, BF), pltpu.VMEM(grads.shape, F32),
+                        pltpu.SemaphoreType.DMA((7 + 4 * res.shape[0] + 2 * STEPS,))],
     )(res, gtok, grads, gains)
 
 
-def split_cols(x):
-    ins = jnp.concatenate([x[:, in_cols(u)] for u in range(2)], axis=1)
-    downs = jnp.concatenate([x[:, down_cols(u)] for u in range(2)], axis=1)
-    return x[:, QO:KO], x[:, KO:VO], x[:, VO:OO], x[:, OO:FO], ins, downs
-
-
 def join_cols(q, k, v, o, i, d):
-    parts = [q, k, v, o]
-    for u in range(2):
+    parts = []
+    for j in range(2):
+        parts += [q[:, j * 128:(j + 1) * 128], k[:, j * 128:(j + 1) * 128]]
+    parts += [v, o]
+    for u in range(STEPS):
         parts += [i[:, u * UNITS:(u + 1) * UNITS], d[:, u * UNITS:(u + 1) * UNITS]]
     return jnp.concatenate(parts, axis=1)
 
@@ -674,8 +717,8 @@
     return res, gtok, gain_a.reshape(width), gain_f.reshape(width), q, k, v, o.T, i, d.T
 
 
-PIECES = ((0, 512), (512, 1024), (1024, 2048), (2048, 3072))
-GPIECES = ((1024, 2048), (2048, 3072), (768, 1024), (512, 768), (0, 512))
+PIECES = ((0, 512), (512, 768), (768, 1024), (1024, 2048), (2048, 3072))
+GPIECES = ((1024, 2048), (2048, 3072), (768, 1024), (512, 768), (0, 256), (256, 512))
 MESH = pl.DeviceIdType.MESH
 ROWS = D // 16
 
@@ -728,12 +771,14 @@
         e = self.e
         if kind in self.fixed:
             return self.fixed[kind][key[0]] + ("t",)
-        if kind in ("z", "x", "y", "d", "xy", "yx", "t"):
+        if kind in ("z", "zz", "x", "y", "d", "xy", "yx", "t"):
             piece, d = key
             cols = slice(*PIECES[piece])
             first, second = halves(*PIECES[piece])
             if kind == "z":
                 at, to = self.w_rows(self.f, 1, cols), d
+            elif kind == "zz":
+                at, to = self.w_rows(self.zi * 4, 4, cols), d
             elif kind == "t":
                 at, to = self.w_rows(self.z_from(d) * 4, 4, cols), "t"
             elif kind == "xy":
@@ -796,7 +841,7 @@
         self.to_plane(piece, 0)
 
     def to_plane(self, piece, d):
-        for k in "xyd" if piece < 2 else "xy":
+        for k in "xyd" if piece < 3 else "xy":
             self.send(k, piece, d)
 
     def plane(self, piece, d):
@@ -813,6 +858,18 @@
         for k in ("x", "y", "d") if piece < 2 else ("xy", "yx"):
             self.arrived(k, piece, d)
         self.send("t", piece, d)
+
+    def turn(self, piece):
+        for k in "xyd":
+            self.arrived(k, piece, 0)
+        for d in (1, 2, 3):
+            self.send("zz", piece, d)
+        self.send("t", piece, 0)
+
+    def turned(self, piece):
+        for d in (1, 2, 3):
+            self.arrived("zz", piece, d)
+            self.send("t", piece, d)
 
     def gathered(self, piece):
         for d in range(4):
@@ -862,11 +919,11 @@
 
     def grads_in(self, piece):
         cols = slice(*GPIECES[piece])
-        for d in (1, 2, 3):
-            self.arrived("gz", piece, d)
+        for n in range(3):
+            self.arrived("gz", piece, n + 1)
         total = self.out[:, cols]
-        for d in range(3):
-            total = total + self.e.rz[d, :, cols].astype(F32)
+        for n in range(3):
+            total = total + self.e.rz[n, :, cols].astype(F32)
         self.out[:, cols] = total
 
     def gains_sum(self, step):
@@ -890,7 +947,7 @@
             return e.gs[2] + e.gr[4] + e.gr[5] + e.gr[6]
 
 
-NSEM = 135
+NSEM = 151
 NSEND = 24
 
 
@@ -934,58 +991,61 @@
     transpose_into(s.nmt, s.nm)
     for d in three:
         link.plane(0, d)
-    link.own_z(2)
+    link.own_z(3)
     transpose_into(s.cott, s.cotp)
     st_bias(s)
     for d in three:
         link.plane(1, d)
+    link.own_plane(3)
+    link.turn(2)
     for d in four:
         link.pair(0, d)
-    link.own_z(3)
+    link.own_z(4)
     link.gathered(0)
     st_query_key(s, w)
-    link.plane(2, 1)
-    link.plane(2, 2)
+    link.plane(3, 1)
+    link.plane(3, 2)
 
     def halfway():
         for d in four:
             link.pair(1, d)
-        link.plane(2, 3)
-        link.own_plane(3)
+        link.plane(3, 3)
+        link.own_plane(4)
     st_sinkhorn(s, seg.at[pl.ds(c, 1), :], halfway)
     link.gathered(1)
     st_values(s, w)
-    link.corner(2, 0)
-    link.corner(2, 1)
-    st_sort(s)
-    link.plane(3, 1)
-    link.corner(2, 2)
-    link.corner(2, 3)
-    st_attend(s, 0)
-    link.plane(3, 2)
-    link.plane(3, 3)
-    link.pair(2, 0)
-    link.pair(2, 1)
-    st_attend(s, 1)
-    link.pair(2, 2)
-    link.pair(2, 3)
     link.corner(3, 0)
     link.corner(3, 1)
+    st_sort(s)
+    link.corner(3, 2)
+    link.corner(3, 3)
+    st_attend(s, 0)
+    link.pair(3, 0)
+    link.pair(3, 1)
+    link.turned(2)
+    link.plane(4, 1)
+    link.plane(4, 2)
+    link.plane(4, 3)
+    st_attend(s, 1)
+    link.pair(3, 2)
+    link.pair(3, 3)
+    link.gathered(2)
     st_out(s, w, gain_ffn)
     transpose_into(s.nft, s.nf)
-    link.gathered(2)
+    link.gathered(3)
 
     def ffn(u):
         early, late = u == 0, u == 1
-        pl.when(late)(lambda: link.gathered(3))
+        @pl.when(late)
+        def _():
+            link.gathered(4)
+
         st_ffn(s, w, 1 - c, u, None)
 
         @pl.when(early)
         def _():
-            link.corner(3, 2)
-            link.corner(3, 3)
-            link.pair(3, 0)
-            link.pair(3, 1)
+            for d in four:
+                link.corner(4, d)
         st_ffn_grads(s, g, None, 1 - c, u, False)
         for n in range(2):
             pl.when(u == n)(functools.partial(link.grads_pair, n))
@@ -993,8 +1053,8 @@
 
         @pl.when(early)
         def _():
-            link.pair(3, 2)
-            link.pair(3, 3)
+            for d in four:
+                link.pair(4, d)
             link.arrived("gt", 0)
 
         @pl.when(late)
@@ -1008,20 +1068,24 @@
     st_mid_back(s, w, gain_ffn)
     st_out_grads(s, g, None, 1 - c, False)
     link.grads_pair(2)
-    link.grads_line(0, False)
-    link.arrived("gt", 2)
-    st_out_grads(s, g, e.other, c, True)
-    link.grads_plane(2)
 
     def attend0():
+        link.arrived("gt", 2)
+        st_out_grads(s, g, e.other, c, True)
+        link.grads_plane(2)
+        link.grads_line(0, False)
+
+    def sort0():
         link.grads_join(1)
 
     def first():
         link.grads_pair(3)
-        link.grads_in(0)
-
-    def sort1():
+
+    def pair():
         link.arrived("gt", 3)
+
+    def queries():
+        link.grads_plane(4)
         link.grads_line(1, False)
 
     def values():
@@ -1029,10 +1093,10 @@
         link.grads_line(2, True)
 
     def last():
-        link.grads_plane(4)
+        link.grads_plane(5)
 
     attention_backward(s, w, g, e.other, c, gain_attn, e.cot, {
-        "attend0": attend0, "first": first, "sort1": sort1, "values": values, "last": last})
+        "attend0": attend0, "sort0": sort0, "first": first, "pair": pair, "queries": queries, "values": values, "last": last})
     e.gs[0] = s.gg[...]
     link.gains_sum(0)
     stores = []
@@ -1041,12 +1105,15 @@
         stores.append(pltpu.make_async_copy(buf.at[mine, :], out.at[c], local.at[2 + n]))
         stores[n].start()
         link.send("out", n)
+    link.grads_line(4, True)
+    link.gains_sum(1)
+    link.grads_in(0)
+    link.grads_in(2)
     link.grads_line(3, True)
-    link.gains_sum(1)
+    link.grads_line(5, True)
+    link.gains_sum(2)
     link.grads_in(1)
-    link.grads_in(2)
-    link.grads_line(4, True)
-    link.gains_sum(2)
+    link.grads_in(4)
     link.grads_in(3)
     link.arrived("out", 0)
     link.arrived("out", 1)
@@ -1056,7 +1123,7 @@
     width = D // 32
     pick = (iota((D, 128), 0) == iota((D, 128), 1) + (2 * f + c) * width).astype(F32)
     gains[...] = nn(total, pick, precision=HI)
-    link.grads_in(4)
+    link.grads_in(5)
     link.finish()
 
 

time: 91.9 us -> 89.6 us (0.975)
  Pallas kernels: 90.9 us -> 88.5 us
    pallas_call x1, Pallas kernels: 86.7 us -> 84.6 us  [by_kernel(): pl.pallas_call(step_kernel, out_shape=(jax.ShapeDtypeStruct(tokens.shape,...]
where the time goes in v1:
time: 89.6 us; the launch traced here: 89.3 us
  Pallas kernels  88.5 us (99%)
    pallas_call x1, Pallas kernels, by_kernel(): pl.pallas_call(step_kernel, out_shape=(jax.ShapeDtypeStruct(tokens.shape,...  84.6 us
    pallas_call x1, Pallas kernels, last_call(): pl.pallas_call(last_kernel, out_shape=(jax.ShapeDtypeStruct(res.shape, BF...  3.83 us

profile of v1, /device:TPU:0, one launch (start us, length us, event | category | flops | bytes accessed | tf_op | source)
XLA Modules:
  0.0 89.3 jit_solution(9732657956399472363)
XLA Ops:
  0.6 84.6 %shard_map.186 = (bf16[2,512,512]{2,1,0:T(8,128)(2,1)}, bf16[2,512,512]{2,1,0:T(8,128)(2,1)}, f32[32,3072]{1,0:T(8,128)}, f32[8,128]{1,0:T(8,128)}) custom-call(bf16[2,512,512]{2,1,0:T(8,128)(2,1)} %tokens.1, bf16[2,512,512]{2,1,0:T(8,128)(2,1)} %cotangent.1, f32[1,512]{1,0:T(1,128)} %bitcast.10, f32[1,512]{1,0:T(1,128)} %bitcast.11, bf16[32,256]{1,0:T(8,128)(2,1)} %wq.1, ...), custom_call_target="tpu_custom_call" | custom-call | tf_op jit(solution)/shard_map/pallas_call | solution.py:1133
  85.3 3.8 %shard_map.187 = (bf16[2,512,512]{2,1,0:T(8,128)(2,1)}, bf16[2,512,512]{2,1,0:T(8,128)(2,1)}, f32[1,16]{1,0:T(1,128)}, f32[1,16]{1,0:T(1,128)}, f32[32,256]{1,0:...) custom-call(bf16[2,512,512]{2,1,0:T(8,128)(2,1)} %get-tuple-element., ...), custom_call_target="tpu_custom_call" | custom-call | tf_op jit(solution)/shard_map/pallas_call | solution.py:678

commit v2 on v1

--- a/solution.py
+++ b/solution.py
@@ -157,23 +157,22 @@
             s.v[rows(m, 256), t * 256:(t + 1) * 256] = nn(x, w[t, :, VO:VO + HALF]).astype(BF)
 
 
-def st_query_key(s, w):
+def st_query_key(s, w, t):
+    cs = half_cols(t)
+
     def product(m, v):
-        x = s.nm[rows(m, 256), :]
-        v["x"] = [nn(x, w[t, :, 0:512]).astype(BF) for t in range(2)]
+        v["x"] = nn(s.nm[rows(m, 256), :], w[t, :, 0:512]).astype(BF)
 
     def store(m, v):
-        at = rows(m, 256)
-        for t, out in enumerate(v.pop("x")):
-            cs = slice(t * 256, (t + 1) * 256)
-            queries = jnp.concatenate([out[:, 0:128], out[:, 256:384]], axis=1)
-            keys = jnp.concatenate([out[:, 128:256], out[:, 384:512]], axis=1)
-            qv, kv = queries.astype(F32), keys.astype(F32)
-            s.q[at, cs] = (qv * (1.0 / math.sqrt(HD))).astype(BF)
-            s.k[at, cs] = keys
-            for ref, val in ((s.qm, qv), (s.km, kv)):
-                sums = jnp.concatenate([block_sums(val[:128]), block_sums(val[128:])], axis=0)
-                ref[rows(m, 8), cs] = sums * (1.0 / BLK)
+        at, out = rows(m, 256), v.pop("x")
+        queries = jnp.concatenate([out[:, 0:128], out[:, 256:384]], axis=1)
+        keys = jnp.concatenate([out[:, 128:256], out[:, 384:512]], axis=1)
+        qv, kv = queries.astype(F32), keys.astype(F32)
+        s.q[at, cs] = (qv * (1.0 / math.sqrt(HD))).astype(BF)
+        s.k[at, cs] = keys
+        for ref, val in ((s.qm, qv), (s.km, kv)):
+            sums = jnp.concatenate([block_sums(val[:128]), block_sums(val[128:])], axis=0)
+            ref[rows(m, 8), cs] = sums * (1.0 / BLK)
     pipeline(range(4), (product, store), (0, 1))
 
 
@@ -604,7 +603,8 @@
     transpose_into(s.cott, s.cotp)
     transpose_into(s.nmt, s.nm)
     st_bias(s)
-    st_query_key(s, w)
+    for t in range(2):
+        st_query_key(s, w, t)
     st_sinkhorn(s, seg)
     st_values(s, w)
     st_sort(s)
@@ -947,7 +947,7 @@
             return e.gs[2] + e.gr[4] + e.gr[5] + e.gr[6]
 
 
-NSEM = 151
+NSEM = 154
 NSEND = 24
 
 
@@ -1001,8 +1001,9 @@
     for d in four:
         link.pair(0, d)
     link.own_z(4)
+    st_query_key(s, w, c)
     link.gathered(0)
-    st_query_key(s, w)
+    st_query_key(s, w, 1 - c)
     link.plane(3, 1)
     link.plane(3, 2)
 
@@ -1029,6 +1030,7 @@
     st_attend(s, 1)
     link.pair(3, 2)
     link.pair(3, 3)
+    link.corner(4, 0)
     link.gathered(2)
     st_out(s, w, gain_ffn)
     transpose_into(s.nft, s.nf)
@@ -1044,7 +1046,7 @@
 
         @pl.when(early)
         def _():
-            for d in four:
+            for d in three:
                 link.corner(4, d)
         st_ffn_grads(s, g, None, 1 - c, u, False)
         for n in range(2):
@@ -1089,7 +1091,7 @@
         link.grads_line(1, False)
 
     def values():
-        link.grads_plane(3)
+        link.grads_part(3)
         link.grads_line(2, True)
 
     def last():
@@ -1097,6 +1099,7 @@
 
     attention_backward(s, w, g, e.other, c, gain_attn, e.cot, {
         "attend0": attend0, "sort0": sort0, "first": first, "pair": pair, "queries": queries, "values": values, "last": last})
+    link.grads_join(3)
     e.gs[0] = s.gg[...]
     link.gains_sum(0)
     stores = []
@@ -1109,9 +1112,9 @@
     link.gains_sum(1)
     link.grads_in(0)
     link.grads_in(2)
-    link.grads_line(3, True)
     link.grads_line(5, True)
     link.gains_sum(2)
+    link.grads_line(3, False)
     link.grads_in(1)
     link.grads_in(4)
     link.grads_in(3)

time: 89.6 us -> 89.2 us (level)
  no operation moved by 1% of the time
where the time goes in v2:
time: 89.2 us; the launch traced here: 89 us
  Pallas kernels  88.1 us (99%)
    pallas_call x1, Pallas kernels, by_kernel(): pl.pallas_call(step_kernel, out_shape=(jax.ShapeDtypeStruct(tokens.shape,...  84.3 us
    pallas_call x1, Pallas kernels, last_call(): pl.pallas_call(last_kernel, out_shape=(jax.ShapeDtypeStruct(res.shape, BF...  3.83 us

profile of v2, /device:TPU:0, one launch (start us, length us, event | category | flops | bytes accessed | tf_op | source)
XLA Modules:
  0.0 89.0 jit_solution(781660124623558897)
XLA Ops:
  0.6 84.3 %shard_map.186 = (bf16[2,512,512]{2,1,0:T(8,128)(2,1)}, bf16[2,512,512]{2,1,0:T(8,128)(2,1)}, f32[32,3072]{1,0:T(8,128)}, f32[8,128]{1,0:T(8,128)}) custom-call(bf16[2,512,512]{2,1,0:T(8,128)(2,1)} %tokens.1, bf16[2,512,512]{2,1,0:T(8,128)(2,1)} %cotangent.1, f32[1,512]{1,0:T(1,128)} %bitcast.10, f32[1,512]{1,0:T(1,128)} %bitcast.11, bf16[32,256]{1,0:T(8,128)(2,1)} %wq.1, ...), custom_call_target="tpu_custom_call" | custom-call | tf_op jit(solution)/shard_map/pallas_call | solution.py:1136
  84.9 3.8 %shard_map.187 = (bf16[2,512,512]{2,1,0:T(8,128)(2,1)}, bf16[2,512,512]{2,1,0:T(8,128)(2,1)}, f32[1,16]{1,0:T(1,128)}, f32[1,16]{1,0:T(1,128)}, f32[32,256]{1,0:...) custom-call(bf16[2,512,512]{2,1,0:T(8,128)(2,1)} %get-tuple-element., ...), custom_call_target="tpu_custom_call" | custom-call | tf_op jit(solution)/shard_map/pallas_call | solution.py:678

commit v3 on v2

--- a/solution.py
+++ b/solution.py
@@ -1011,7 +1011,6 @@
         for d in four:
             link.pair(1, d)
         link.plane(3, 3)
-        link.own_plane(4)
     st_sinkhorn(s, seg.at[pl.ds(c, 1), :], halfway)
     link.gathered(1)
     st_values(s, w)
@@ -1020,6 +1019,7 @@
     st_sort(s)
     link.corner(3, 2)
     link.corner(3, 3)
+    link.own_plane(4)
     st_attend(s, 0)
     link.pair(3, 0)
     link.pair(3, 1)

time: 89.2 us -> 89.3 us (level)
  no operation moved by 1% of the time
where the time goes in v3:
time: 89.3 us; the launch traced here: 89.1 us
  Pallas kernels  88.2 us (99%)
    pallas_call x1, Pallas kernels, by_kernel(): pl.pallas_call(step_kernel, out_shape=(jax.ShapeDtypeStruct(tokens.shape,...  84.4 us
    pallas_call x1, Pallas kernels, last_call(): pl.pallas_call(last_kernel, out_shape=(jax.ShapeDtypeStruct(res.shape, BF...  3.83 us

profile of v3, /device:TPU:0, one launch (start us, length us, event | category | flops | bytes accessed | tf_op | source)
XLA Modules:
  0.0 89.1 jit_solution(4688295070364945465)
XLA Ops:
  0.6 84.4 %shard_map.186 = (bf16[2,512,512]{2,1,0:T(8,128)(2,1)}, bf16[2,512,512]{2,1,0:T(8,128)(2,1)}, f32[32,3072]{1,0:T(8,128)}, f32[8,128]{1,0:T(8,128)}) custom-call(bf16[2,512,512]{2,1,0:T(8,128)(2,1)} %tokens.1, bf16[2,512,512]{2,1,0:T(8,128)(2,1)} %cotangent.1, f32[1,512]{1,0:T(1,128)} %bitcast.10, f32[1,512]{1,0:T(1,128)} %bitcast.11, bf16[32,256]{1,0:T(8,128)(2,1)} %wq.1, ...), custom_call_target="tpu_custom_call" | custom-call | tf_op jit(solution)/shard_map/pallas_call | solution.py:1136
  85.0 3.8 %shard_map.187 = (bf16[2,512,512]{2,1,0:T(8,128)(2,1)}, bf16[2,512,512]{2,1,0:T(8,128)(2,1)}, f32[1,16]{1,0:T(1,128)}, f32[1,16]{1,0:T(1,128)}, f32[32,256]{1,0:...) custom-call(bf16[2,512,512]{2,1,0:T(8,128)(2,1)} %get-tuple-element., ...), custom_call_target="tpu_custom_call" | custom-call | tf_op jit(solution)/shard_map/pallas_call | solution.py:678
